TPU v7x, 128 devices: a whole 4x4x4 slice. The times are simulated.
128 devices in a mesh: row: 8 (over y, core), col: 16 (over z, x).
Axes of the slice: x: 4, y: 4, z: 4, core: 2. Of those that a mesh axis runs over, the one named last changes fastest.
Arguments:
- ancestor_inverse: float32 [12288, 12288], P('row', 'col')
- factor: bfloat16 [3, 12288, 512], P(None, ('row', 'col')), may hold values from -0.5 to 0.5
- coupling: float32 [3, 512, 512], replicated, may hold values from -0.25 to 0.25
- diagonal_inverse: float32 [3, 512, 512], replicated, may hold values from -6 to 6
- ancestors: int32 [3, 24], replicated, may hold values from -1 to 23, as said below
Outputs:
- block_columns: float32 [3, 12288, 512], P(None, ('row', 'col'))
- block_rows: float32 [3, 12288, 512], P(None, ('col', 'row'))
- node_blocks: float32 [3, 3, 512, 512], replicated
Inputs may be any that keep to these rules, and one draw needn't show every extreme that they name: `ancestors`: row k lists the ancestor block rows of supernode k, blocks of 512 rows: distinct indices in increasing order, then -1 in the slots left. Every block is listed by some supernode.
All inputs are finite; a program needn't handle non-finite values.
Results may differ from a plain program's by a relative error of at most 0.0003.
Values may be sent and summed in bfloat16 or wider, within the bound.
A program may use at most 128 MiB of HBM per device.

v0:
```python
import jax
import jax.numpy as jnp
from jax import lax
from jax.sharding import PartitionSpec as P

highest = lax.Precision.HIGHEST


def broadcast(value, axis, source):
    kept = jnp.where(lax.axis_index(axis) == source, value, 0).astype(value.dtype)
    return lax.psum(kept, axis)


def matmul(left, right):
    return jnp.dot(left, right, precision=highest)


def left_dot(left, right):
    return lax.dot_general(left, right, (((0,), (0,)), ((), ())), precision=highest)


def pair_index(later, earlier):
    return later * (later - 1) // 2 + earlier


def local(ancestor_inverse, factor, coupling, diagonal_inverse, ancestors):
    col_count = lax.axis_size("col")
    row_count = lax.axis_size("row")
    row_index = lax.axis_index("row")
    col_index = lax.axis_index("col")
    nodes_total, piece_rows, sn_width = factor.shape
    rows_here, cols_here = ancestor_inverse.shape
    group_ratio = rows_here // cols_here
    first_row = (row_index * col_count + col_index) * piece_rows
    block_of_row = (first_row + jnp.arange(piece_rows, dtype=jnp.int32)) // sn_width
    source_row = col_index // group_ratio
    block_start = col_index % group_ratio * cols_here
    row_layout = []
    solved = {}
    for current in range(nodes_total):
        listed = jnp.any(ancestors[current][:, None] == block_of_row[None, :], axis=0)
        lower_part = jnp.where(listed[:, None], factor[current], jnp.zeros_like(factor[current]))
        lower_rows = lax.all_gather(lower_part, "col", axis=0, tiled=True)
        own_block = lax.dynamic_slice_in_dim(lower_rows, block_start, cols_here, 0)
        lower_cols = broadcast(own_block, "row", source_row).astype(jnp.float32)
        lower_here = lower_part.astype(jnp.float32)
        product_sum = lax.psum_scatter(
            matmul(ancestor_inverse, lower_cols), "col", scatter_dimension=0, tiled=True
        )
        for earlier in range(current):
            product_sum = product_sum + matmul(
                row_layout[earlier], coupling[pair_index(current, earlier)]
            )
        column = -product_sum
        stacked = jnp.concatenate(row_layout + [column], axis=1)
        summed = lax.psum(left_dot(lower_here, stacked), ("row", "col"))
        crosses = [
            summed[:, earlier * sn_width : (earlier + 1) * sn_width] for earlier in range(current)
        ]
        self_term = summed[:, current * sn_width : (current + 1) * sn_width]
        for earlier in range(current):
            block_value = -crosses[earlier].T
            for inner in range(current):
                block_value = block_value - matmul(
                    solved[earlier, inner], coupling[pair_index(current, inner)]
                )
            solved[earlier, current] = block_value
            solved[current, earlier] = block_value.T
        diag_value = diagonal_inverse[current] - self_term
        for earlier in range(current):
            diag_value = diag_value - left_dot(
                coupling[pair_index(current, earlier)], solved[earlier, current]
            )
        solved[current, current] = diag_value
        row_layout.append(column)
    finished = jnp.stack(row_layout)
    part_rows = piece_rows // row_count
    ratio_cols = col_count // row_count
    split_parts = finished.reshape(nodes_total, row_count, part_rows, sn_width)
    held = lax.all_to_all(split_parts, "row", split_axis=1, concat_axis=1, tiled=True)
    targets = jnp.arange(row_count, dtype=jnp.int32) * ratio_cols + col_index // row_count
    onehot = (targets[:, None] == jnp.arange(col_count, dtype=jnp.int32)[None, :]).astype(
        jnp.float32
    )
    slotted = jnp.einsum("rc,nrqs->ncqs", onehot, held, precision=highest)
    arrived = lax.all_to_all(slotted, "col", split_axis=1, concat_axis=1, tiled=True)
    picked = lax.dynamic_slice_in_dim(arrived, col_index % ratio_cols * row_count, row_count, 1)
    landed = lax.all_to_all(picked, "row", split_axis=1, concat_axis=1, tiled=True)
    mirrored_all = landed.reshape(nodes_total, piece_rows, sn_width)
    node_blocks = jnp.stack(
        [
            jnp.stack([solved[first_node, second_node] for second_node in range(nodes_total)])
            for first_node in range(nodes_total)
        ]
    )
    return (finished, mirrored_all, node_blocks)


def solution(mesh):
    placed = (P("row", "col"), P(None, ("row", "col"), None), P(), P(), P())
    return jax.shard_map(
        local,
        mesh=mesh,
        in_specs=placed,
        out_specs=(P(None, ("row", "col"), None), P(None, ("col", "row"), None), P()),
        check_vma=False,
    )
```

profile of v0, /device:TPU:1, one launch (start us, length us, event | category | flops | bytes accessed | tf_op | source)
XLA Modules:
  0.0 691.0 jit_solution(10552824575240240170)
XLA Ops:
  7.2 0.8 slice_bitcast_fusion.2
  8.1 1.8 bitcast_select_fusion.1
  10.0 0.7 all-gather.4.cloned.1.call-update
  11.5 45.6 %all-gather.6.cloned.1.call-done = bf16[1536,512]{1,0:T(8,128)(2,1)} async-done(((bf16[96,512]{1,0:T(8,128)(2,1)}), bf16[1536,512]{1,0:T(8,128)(2,1)}) %all-gather.6.cloned.1.call-update) | async-done | bytes 1572880 | tf_op jit(solution)/shard_map/all_gather | solution.py:43
  57.1 2.2 dynamic-slice_select_fusion.1
  59.2 43.3 %all-gather.4.cloned.1.call-done = bf16[1536,512]{1,0:T(8,128)(2,1)} async-done(((bf16[96,512]{1,0:T(8,128)(2,1)}), bf16[1536,512]{1,0:T(8,128)(2,1)}) %all-gather.4.cloned.1.call-update) | async-done | bytes 1572880 | tf_op jit(solution)/shard_map/all_gather | solution.py:43
  102.5 2.1 dynamic-slice_select_fusion.2
  104.7 43.3 %all-gather.8.cloned.1.call-done = bf16[1536,512]{1,0:T(8,128)(2,1)} async-done(((bf16[96,512]{1,0:T(8,128)(2,1)}), bf16[1536,512]{1,0:T(8,128)(2,1)}) %all-gather.8.cloned.1.call-update) | async-done | bytes 1572880 | tf_op jit(solution)/shard_map/all_gather | solution.py:43
  148.0 2.1 dynamic-slice_select_fusion
  150.3 66.0 %all-reduce.7.cloned.1.call-done = (bf16[768,512]{1,0:T(8,128)(2,1)}, bf16[768,512]{1,0:T(8,128)(2,1)}, bf16[768,512]{1,0:T(8,128)(2,1)}) async-done(((bf16[768,512]{1,0:T(8,128)(2,1)}, bf16[768,512]{1,0:T(8,128)(2,1)}, bf16[768,512]{1,0:T(8,128)(2,1)}), (bf16[768,512]{1,0:T(8,128)(2,1)}, bf16[768,512]{1,0:T(8,128)(2,1)}, bf16[768,512]{1,0:T(8,128)(2,1)})) %all-reduce.7.cloned.1.call-update) | async-done | bytes 2359312 | tf_op jit(solution)/shard_map/psum | solution.py:11
  216.2 6.7 convolution_bitcast_fusion.2
  222.9 2.3 copy.104
  225.3 6.7 convolution_bitcast_fusion.1
  232.0 2.4 copy.106
  234.5 6.7 convolution_bitcast_fusion
  241.2 2.4 copy.108
  244.1 57.1 %reduce-scatter.10.cloned.1.call-done = f32[96,512]{1,0:T(8,128)} async-done(((f32[1536,512]{1,0:T(8,128)}), f32[96,512]{1,0:T(8,128)}) %reduce-scatter.10.cloned.1.call-update) | async-done | bytes 196624 | tf_op jit(solution)/shard_map/reduce_scatter | solution.py:47
  301.2 78.3 %reduce-scatter.12.cloned.1.call-done = f32[96,512]{1,0:T(8,128)} async-done(((f32[1536,512]{1,0:T(8,128)}), f32[96,512]{1,0:T(8,128)}) %reduce-scatter.12.cloned.1.call-update) | async-done | bytes 196624 | tf_op jit(solution)/shard_map/reduce_scatter | solution.py:47
  379.5 1.8 fusion.5
  381.3 77.3 %reduce-scatter.14.cloned.1.call-done = f32[96,512]{1,0:T(8,128)} async-done(((f32[1536,512]{1,0:T(8,128)}), f32[96,512]{1,0:T(8,128)}) %reduce-scatter.14.cloned.1.call-update) | async-done | bytes 196624 | tf_op jit(solution)/shard_map/reduce_scatter | solution.py:47
  458.6 1.8 convolution_add_fusion.1
  460.4 0.7 fusion.4
  461.2 0.7 fusion.63
  461.9 2.3 fusion.45
  464.2 3.1 fusion.38
  467.4 1.6 fusion.54
  469.0 0.9 copy-done.18
  469.9 0.7 stack.74
  470.6 0.7 stack.73
  471.4 1.6 stack.72
  473.0 1.2 pad_maximum_fusion.1
  474.2 1.0 copy.78
  475.2 6.7 all-to-all-start
  481.9 15.6 %all-to-all-done = f32[3,8,12,512]{3,2,0,1:T(8,128)} async-done(((f32[3,8,12,512]{3,2,0,1:T(8,128)}), f32[3,8,12,512]{3,2,0,1:T(8,128)}, u32[]{:S(2)}, u32[]{:S(2)}) %all-to-all-start) | async-done | bytes 589856 | tf_op jit(solution)/shard_map/all_to_all | solution.py:80
  497.5 2.1 convolution_bitcast_fusion.3
  499.6 1.9 copy.80
  501.5 4.8 all-to-all-start.1
  506.3 21.0 %all-to-all-done.1 = f32[3,16,12,512]{3,2,0,1:T(8,128)} async-done(((f32[3,16,12,512]{3,2,0,1:T(8,128)}), f32[3,16,12,512]{3,2,0,1:T(8,128)}, u32[]{:S(2)}, u32[]{:S(2)}) %all-to-all-start.1) | async-done | bytes 1179680 | tf_op jit(solution)/shard_map/all_to_all | solution.py:86
  527.3 2.1 constant_dynamic-slice_fusion
  529.4 9.0 %all-to-all-start.2 = ((f32[3,8,12,512]{3,2,0,1:T(8,128)}), f32[3,8,12,512]{3,2,0,1:T(8,128)}, u32[]{:S(2)}, u32[]{:S(2)}) async-start(f32[3,8,12,512]{3,2,0,1:T(8,128)} %constant_dynamic-slice_fusion), calls=%async_computation.2 | async-start | bytes 1572864 | tf_op jit(solution)/shard_map/all_to_all | solution.py:88
  538.4 2.4 slice.71
  540.8 2.6 copy.110
  543.4 1.8 pad_maximum_fusion.2
  545.1 5.7 all-to-all-done.2
  550.9 2.2 copy.81
  553.0 2.0 reshape.46
  555.1 83.9 %all-reduce.5.cloned.1.call-done = (f32[512,1536]{1,0:T(8,128)}, f32[512,512]{1,0:T(8,128)}, f32[512,1024]{0,1:T(8,128)}) async-done(((f32[512,1536]{1,0:T(8,128)}, f32[512,512]{1,0:T(8,128)}, f32[512,1024]{0,1:T(8,128)}), (f32[512,1536]{1,0:T(8,128)}, f32[512,512]{1,0:T(8,128)}, f32[512,1024]{0,1:T(8,128)})) %all-reduce.5.cloned.1.call-update) | async-done | bytes 6291472 | tf_op jit(solution)/shard_map/psum | solution.py:56
  638.9 3.8 bitcast_subtract_fusion.7
  642.7 1.9 fusion.14
  644.6 1.9 fusion.18
  646.6 1.9 fusion.20
  648.5 2.0 fusion.3
  650.5 1.0 copy-done.7
  651.5 2.1 fusion.12
  653.7 3.1 fusion.2
  656.8 2.3 fusion.7
  659.1 2.3 fusion.60
  661.4 2.6 copy.85
  663.9 3.8 maximum_bitcast_fusion.1
  667.8 3.6 copy.95
  671.3 4.3 fusion.1
  676.0 0.9 copy-done.13
  677.5 1.6 copy-done.5
  679.1 4.9 pad_maximum_fusion
  (62 shorter events, 2.7 us)
Async XLA Ops:
  7.2 49.9 %all-gather.6.cloned.1.call-start = ((), (), s32[]{:S(2)}) async-start(), calls=%async_computation.7 | async-start | bytes 1671168 | tf_op jit(solution)/shard_map/all_gather | solution.py:43
  9.9 92.6 %all-gather.4.cloned.1.call-start = ((), (), s32[]{:S(2)}) async-start(), calls=%async_computation.6 | async-start | bytes 1671168 | tf_op jit(solution)/shard_map/all_gather | solution.py:43
  10.7 137.4 %all-gather.8.cloned.1.call-start = ((), (), s32[]{:S(2)}) async-start(), calls=%async_computation.8 | async-start | bytes 1671168 | tf_op jit(solution)/shard_map/all_gather | solution.py:43
  11.4 204.8 %all-reduce.7.cloned.1.call-start = ((), (), s32[]{:S(2)}) async-start(), calls=%async_computation.13 | async-start | bytes 4718592 | tf_op jit(solution)/shard_map/psum | solution.py:11
  150.2 151.0 %reduce-scatter.10.cloned.1.call-start = ((), (), s32[]{:S(2)}) async-start(), calls=%async_computation.9 | async-start | bytes 3342336 | tf_op jit(solution)/shard_map/reduce_scatter | solution.py:47
  225.3 154.3 %reduce-scatter.12.cloned.1.call-start = ((), (), s32[]{:S(2)}) async-start(), calls=%async_computation.10 | async-start | bytes 3342336 | tf_op jit(solution)/shard_map/reduce_scatter | solution.py:47
  234.4 224.1 %reduce-scatter.14.cloned.1.call-start = ((), (), s32[]{:S(2)}) async-start(), calls=%async_computation.11 | async-start | bytes 3342336 | tf_op jit(solution)/shard_map/reduce_scatter | solution.py:47
  243.6 136.0 %copy-start = (f32[3,512,512]{2,1,0:T(8,128)S(1)}, f32[3,512,512]{2,1,0:T(8,128)}, u32[]{:S(2)}) copy-start(f32[3,512,512]{2,1,0:T(8,128)} %param.7) | copy-start | bytes 9437188
  243.6 395.3 %all-reduce.5.cloned.1.call-start = ((), (), s32[]{:S(2)}) async-start(), calls=%async_computation.12 | async-start | bytes 12582912 | tf_op jit(solution)/shard_map/psum | solution.py:56
  301.2 159.9 %copy-start.16 = (f32[96,512]{1,0:T(8,128)S(1)}, f32[96,512]{1,0:T(8,128)}, u32[]{:S(2)}) copy-start(f32[96,512]{1,0:T(8,128)} %reduce-scatter.10.cloned.1.call-done) | copy-start | bytes 589828
  458.6 3.3 copy-start.20
  458.6 5.7 copy-start.22
  461.1 6.2 copy-start.17
  461.9 5.5 copy-start.19
  461.9 5.5 copy-start.21
  469.0 0.9 copy-start.18
  475.2 22.3 %all-to-all-start = ((f32[3,8,12,512]{3,2,0,1:T(8,128)}), f32[3,8,12,512]{3,2,0,1:T(8,128)}, u32[]{:S(2)}, u32[]{:S(2)}) async-start(f32[3,8,12,512]{3,2,0,1:T(8,128)} %copy.78), calls=%async_computation | async-start | bytes 1572864 | tf_op jit(solution)/shard_map/all_to_all | solution.py:80
  501.5 25.8 %all-to-all-start.1 = ((f32[3,16,12,512]{3,2,0,1:T(8,128)}), f32[3,16,12,512]{3,2,0,1:T(8,128)}, u32[]{:S(2)}, u32[]{:S(2)}) async-start(f32[3,16,12,512]{3,2,0,1:T(8,128)} %copy.80), calls=%async_computation.1 | async-start | bytes 3145728 | tf_op jit(solution)/shard_map/all_to_all | solution.py:86
  529.4 21.4 %all-to-all-start.2 = ((f32[3,8,12,512]{3,2,0,1:T(8,128)}), f32[3,8,12,512]{3,2,0,1:T(8,128)}, u32[]{:S(2)}, u32[]{:S(2)}) async-start(f32[3,8,12,512]{3,2,0,1:T(8,128)} %constant_dynamic-slice_fusion), calls=%async_computation.2 | async-start | bytes 1572864 | tf_op jit(solution)/shard_map/all_to_all | solution.py:88
  642.7 5.8 copy-start.1
  642.7 3.8 copy-start.8
  642.7 3.8 copy-start.9
  644.6 3.9 copy-start.10
  644.6 3.9 copy-start.11
  646.6 12.5 %copy-start.3 = (f32[512,512]{0,1:T(8,128)}, f32[512,512]{0,1:T(8,128)S(1)}, u32[]{:S(2)}) copy-start(f32[512,512]{0,1:T(8,128)S(1)} %fusion.18) | copy-start | bytes 3145732
  648.5 5.1 copy-start.6
  650.5 1.0 copy-start.7
  653.7 5.4 copy-start.4
  671.3 4.3 copy-start.2
  671.3 4.3 copy-start.12
  671.3 4.3 copy-start.15
  675.7 1.2 copy-start.13
  675.7 1.5 copy-start.14
  677.2 1.9 copy-start.5
Sparse Core Ops, SparseCore 0:
  10.7 46.3 all-gather.5
  59.2 43.3 all-gather.3
  104.7 43.3 all-gather.7
  151.0 65.1 all-reduce.6
  225.4 75.7 reduce-scatter.9
  304.4 75.1 reduce-scatter.11
  383.4 75.0 reduce-scatter.13
  469.1 169.7 all-reduce.4
where the time goes:
time: 699 us; the launch traced here: 691 us
  waiting for transfers between devices  539 us (77%)
  matrix products  54.5 us (8%)
  local copies, waits for them, and re-layouts  36 us (5%)
  other arithmetic  26 us (4%)
  starting transfers between devices  21.2 us (3%)
  between operations  14.7 us (2%)
    reduce_scatter x3, waiting for transfers between devices, local(): lax.psum_scatter(matmul(ancestor_inverse, lower_cols), 'col', scatter_dim...  213 us
    all_gather x3, waiting for transfers between devices, local(): lower_rows = lax.all_gather(lower_part, 'col', axis=0, tiled=True)  132 us
    psum x1, waiting for transfers between devices, local(): summed = lax.psum(left_dot(lower_here, stacked), ('row', 'col'))  83.9 us
    psum x1, waiting for transfers between devices, broadcast(): return lax.psum(kept, axis)  66 us
    dot_general x11, matrix products, matmul(): return jnp.dot(left, right, precision=highest)  36 us
    all_to_all x1, waiting for transfers between devices, local(): lax.all_to_all(slotted, 'col', split_axis=1, concat_axis=1, tiled=True)  21 us
    dot_general x6, matrix products, left_dot(): lax.dot_general(left, right, (((0,), (0,)), ((), ())), precision=highest)  16.5 us
    all_to_all x1, waiting for transfers between devices, local(): lax.all_to_all(split_parts, 'row', split_axis=1, concat_axis=1, tiled=True)  15.6 us
  transfers between devices with their start and end apart: 11, of which 11 were waited for; matrix products, arithmetic and copies ran while one was open for 7% of the time, Pallas kernels for 0%

commit v1 on v0

--- a/solution.py
+++ b/solution.py
@@ -83,7 +83,11 @@
         jnp.float32
     )
     slotted = jnp.einsum("rc,nrqs->ncqs", onehot, held, precision=highest)
-    arrived = lax.all_to_all(slotted, "col", split_axis=1, concat_axis=1, tiled=True)
+    z2 = lax.psum(1, "col")
+    block_next = jnp.split(slotted, z2, 1)
+    block_last = jnp.stack(block_next, 0)
+    y = lax.all_to_all(block_last, "col", 0, 0)
+    arrived = jnp.concatenate(y, 1)
     picked = lax.dynamic_slice_in_dim(arrived, col_index % ratio_cols * row_count, row_count, 1)
     landed = lax.all_to_all(picked, "row", split_axis=1, concat_axis=1, tiled=True)
     mirrored_all = landed.reshape(nodes_total, piece_rows, sn_width)

time: 699 us -> 707 us (1.011)
  local copies, waits for them, and re-layouts: 36 us -> 45.5 us
    psum x1, waiting for transfers between devices: 83.9 us -> 98.9 us  [local(): summed = lax.psum(left_dot(lower_here, stacked), ('row', 'col'))]
    all_to_all x1, waiting for transfers between devices: 15.6 us -> 5.74 us  [local(): lax.all_to_all(split_parts, 'row', split_axis=1, concat_axis=1, tiled=True)]
    unnamed x50 -> x55, local copies, waits for them, and re-layouts: 14.4 us -> 23.9 us
    reduce_scatter x3, waiting for transfers between devices: 213 us -> 205 us  [local(): lax.psum_scatter(matmul(ancestor_inverse, lower_cols), 'col', scatter_dim...]
  transfers between devices with their start and end apart: 11 -> 11, of which waited for: 11 -> 11; matrix products, arithmetic and copies ran while one was open for 7% -> 9% of each run, Pallas kernels for 0% -> 0%
where the time goes in v1:
time: 707 us; the launch traced here: 700 us
  waiting for transfers between devices  537 us (76%)
  matrix products  58.1 us (8%)
  local copies, waits for them, and re-layouts  45.5 us (6%)
  other arithmetic  27 us (4%)
  starting transfers between devices  18.3 us (3%)
  between operations  14.7 us (2%)
    reduce_scatter x3, waiting for transfers between devices, local(): lax.psum_scatter(matmul(ancestor_inverse, lower_cols), 'col', scatter_dim...  205 us
    all_gather x3, waiting for transfers between devices, local(): lower_rows = lax.all_gather(lower_part, 'col', axis=0, tiled=True)  132 us
    psum x1, waiting for transfers between devices, local(): summed = lax.psum(left_dot(lower_here, stacked), ('row', 'col'))  98.9 us
    psum x1, waiting for transfers between devices, broadcast(): return lax.psum(kept, axis)  66 us
    dot_general x11, matrix products, matmul(): return jnp.dot(left, right, precision=highest)  36.6 us
    unnamed x55, local copies, waits for them, and re-layouts  23.9 us
    all_to_all x1, waiting for transfers between devices, local(): y = lax.all_to_all(block_last, 'col', 0, 0)  20.8 us
    dot_general x6, matrix products, left_dot(): lax.dot_general(left, right, (((0,), (0,)), ((), ())), precision=highest)  19.4 us
  transfers between devices with their start and end apart: 11, of which 11 were waited for; matrix products, arithmetic and copies ran while one was open for 9% of the time, Pallas kernels for 0%

profile of v1, /device:TPU:1, one launch (start us, length us, event | category | flops | bytes accessed | tf_op | source)
XLA Modules:
  0.0 700.5 jit_solution(2018891398065626859)
XLA Ops:
  7.2 0.8 slice_bitcast_fusion.18
  8.1 1.8 bitcast_select_fusion.1
  11.5 45.6 %all-gather.6.cloned.1.call-done = bf16[1536,512]{1,0:T(8,128)(2,1)} async-done(((bf16[96,512]{1,0:T(8,128)(2,1)}), bf16[1536,512]{1,0:T(8,128)(2,1)}) %all-gather.6.cloned.1.call-update) | async-done | bytes 1572880 | tf_op jit(solution)/shard_map/all_gather | solution.py:43
  57.1 2.2 dynamic-slice_select_fusion.1
  59.3 43.3 %all-gather.4.cloned.1.call-done = bf16[1536,512]{1,0:T(8,128)(2,1)} async-done(((bf16[96,512]{1,0:T(8,128)(2,1)}), bf16[1536,512]{1,0:T(8,128)(2,1)}) %all-gather.4.cloned.1.call-update) | async-done | bytes 1572880 | tf_op jit(solution)/shard_map/all_gather | solution.py:43
  102.5 2.1 dynamic-slice_select_fusion.2
  104.7 43.4 %all-gather.8.cloned.1.call-done = bf16[1536,512]{1,0:T(8,128)(2,1)} async-done(((bf16[96,512]{1,0:T(8,128)(2,1)}), bf16[1536,512]{1,0:T(8,128)(2,1)}) %all-gather.8.cloned.1.call-update) | async-done | bytes 1572880 | tf_op jit(solution)/shard_map/all_gather | solution.py:43
  148.0 2.1 dynamic-slice_select_fusion
  150.3 66.0 %all-reduce.7.cloned.1.call-done = (bf16[768,512]{1,0:T(8,128)(2,1)}, bf16[768,512]{1,0:T(8,128)(2,1)}, bf16[768,512]{1,0:T(8,128)(2,1)}) async-done(((bf16[768,512]{1,0:T(8,128)(2,1)}, bf16[768,512]{1,0:T(8,128)(2,1)}, bf16[768,512]{1,0:T(8,128)(2,1)}), (bf16[768,512]{1,0:T(8,128)(2,1)}, bf16[768,512]{1,0:T(8,128)(2,1)}, bf16[768,512]{1,0:T(8,128)(2,1)})) %all-reduce.7.cloned.1.call-update) | async-done | bytes 2359312 | tf_op jit(solution)/shard_map/psum | solution.py:11
  216.2 6.7 convolution_bitcast_fusion.2
  222.9 2.3 copy.108
  225.3 6.7 convolution_bitcast_fusion.1
  232.0 2.4 copy.110
  234.9 6.8 convolution_bitcast_fusion
  241.8 2.4 copy.112
  244.2 57.0 %reduce-scatter.10.cloned.1.call-done = f32[96,512]{1,0:T(8,128)} async-done(((f32[1536,512]{1,0:T(8,128)}), f32[96,512]{1,0:T(8,128)}) %reduce-scatter.10.cloned.1.call-update) | async-done | bytes 196624 | tf_op jit(solution)/shard_map/reduce_scatter | solution.py:47
  301.2 78.3 %reduce-scatter.12.cloned.1.call-done = f32[96,512]{1,0:T(8,128)} async-done(((f32[1536,512]{1,0:T(8,128)}), f32[96,512]{1,0:T(8,128)}) %reduce-scatter.12.cloned.1.call-update) | async-done | bytes 196624 | tf_op jit(solution)/shard_map/reduce_scatter | solution.py:47
  379.6 1.8 fusion.5
  381.3 0.7 stack.124
  382.0 1.7 fusion.79
  383.8 1.6 stack.123
  385.4 3.4 fusion.45
  388.8 69.8 %reduce-scatter.14.cloned.1.call-done = f32[96,512]{1,0:T(8,128)} async-done(((f32[1536,512]{1,0:T(8,128)}), f32[96,512]{1,0:T(8,128)}) %reduce-scatter.14.cloned.1.call-update) | async-done | bytes 196624 | tf_op jit(solution)/shard_map/reduce_scatter | solution.py:47
  458.6 1.7 convolution_add_fusion.1
  460.3 1.4 fusion.4
  461.7 1.6 stack.125
  463.3 1.2 pad_maximum_fusion.1
  464.5 1.0 copy.80
  465.5 6.7 all-to-all-start
  472.2 2.5 fusion.70
  474.7 4.2 fusion.38
  478.9 5.7 all-to-all-done
  484.6 2.1 convolution_bitcast_fusion.3
  487.4 0.7 fusion.63
  493.6 0.7 fusion.54
  497.8 4.6 all-to-all-start.1
  502.4 20.8 %all-to-all-done.1 = f32[16,3,1,12,512]{4,2,3,1,0:T(1,128)} async-done(((f32[16,3,1,12,512]{4,2,3,1,0:T(1,128)}), f32[16,3,1,12,512]{4,2,3,1,0:T(1,128)}, u32[]{:S(2)}, u32[]{:S(2)}) %all-to-all-start.1) | async-done | bytes 1179680 | tf_op jit(solution)/shard_map/all_to_all | solution.py:89
  523.1 1.5 dynamic-slice_bitcast_fusion
  524.6 1.0 copy.118
  525.6 6.3 all-to-all-start.2
  531.9 2.4 slice.71
  534.3 2.6 copy.114
  536.9 1.8 pad_maximum_fusion.2
  538.7 6.6 all-to-all-done.2
  545.3 2.2 copy.84
  547.5 2.0 reshape.49
  549.5 98.9 %all-reduce.5.cloned.1.call-done = (f32[512,1536]{1,0:T(8,128)}, f32[512,512]{1,0:T(8,128)}, f32[512,1024]{0,1:T(8,128)}) async-done(((f32[512,1536]{1,0:T(8,128)}, f32[512,512]{1,0:T(8,128)}, f32[512,1024]{0,1:T(8,128)}), (f32[512,1536]{1,0:T(8,128)}, f32[512,512]{1,0:T(8,128)}, f32[512,1024]{0,1:T(8,128)})) %all-reduce.5.cloned.1.call-update) | async-done | bytes 6291472 | tf_op jit(solution)/shard_map/psum | solution.py:56
  648.4 3.8 bitcast_subtract_fusion.7
  652.2 1.9 fusion.14
  654.1 1.9 fusion.18
  656.1 1.9 fusion.20
  658.0 2.0 fusion.3
  660.0 1.0 copy-done.7
  661.0 2.1 fusion.12
  663.1 3.1 fusion.2
  666.2 2.3 fusion.7
  668.5 2.3 fusion.76
  670.8 2.5 copy.88
  673.4 3.8 maximum_bitcast_fusion.1
  677.2 3.6 copy.98
  680.8 4.3 fusion.1
  685.4 0.9 copy-done.13
  687.0 1.6 copy-done.5
  688.5 4.9 pad_maximum_fusion
  (68 shorter events, 13.0 us)
Async XLA Ops:
  7.2 49.9 %all-gather.6.cloned.1.call-start = ((), (), s32[]{:S(2)}) async-start(), calls=%async_computation.7 | async-start | bytes 1671168 | tf_op jit(solution)/shard_map/all_gather | solution.py:43
  9.9 92.6 %all-gather.4.cloned.1.call-start = ((), (), s32[]{:S(2)}) async-start(), calls=%async_computation.6 | async-start | bytes 1671168 | tf_op jit(solution)/shard_map/all_gather | solution.py:43
  10.7 137.4 %all-gather.8.cloned.1.call-start = ((), (), s32[]{:S(2)}) async-start(), calls=%async_computation.8 | async-start | bytes 1671168 | tf_op jit(solution)/shard_map/all_gather | solution.py:43
  11.4 204.8 %all-reduce.7.cloned.1.call-start = ((), (), s32[]{:S(2)}) async-start(), calls=%async_computation.13 | async-start | bytes 4718592 | tf_op jit(solution)/shard_map/psum | solution.py:11
  150.2 151.0 %reduce-scatter.10.cloned.1.call-start = ((), (), s32[]{:S(2)}) async-start(), calls=%async_computation.9 | async-start | bytes 3342336 | tf_op jit(solution)/shard_map/reduce_scatter | solution.py:47
  225.3 154.3 %reduce-scatter.12.cloned.1.call-start = ((), (), s32[]{:S(2)}) async-start(), calls=%async_computation.10 | async-start | bytes 3342336 | tf_op jit(solution)/shard_map/reduce_scatter | solution.py:47
  234.4 224.2 %reduce-scatter.14.cloned.1.call-start = ((), (), s32[]{:S(2)}) async-start(), calls=%async_computation.11 | async-start | bytes 3342336 | tf_op jit(solution)/shard_map/reduce_scatter | solution.py:47
  244.1 135.4 %copy-start = (f32[3,512,512]{2,1,0:T(8,128)S(1)}, f32[3,512,512]{2,1,0:T(8,128)}, u32[]{:S(2)}) copy-start(f32[3,512,512]{2,1,0:T(8,128)} %param.7) | copy-start | bytes 9437188
  301.2 157.4 %copy-start.16 = (f32[96,512]{1,0:T(8,128)S(1)}, f32[96,512]{1,0:T(8,128)}, u32[]{:S(2)}) copy-start(f32[96,512]{1,0:T(8,128)} %reduce-scatter.10.cloned.1.call-done) | copy-start | bytes 589828
  465.5 19.1 %all-to-all-start = ((f32[3,8,12,512]{3,2,0,1:T(8,128)}), f32[3,8,12,512]{3,2,0,1:T(8,128)}, u32[]{:S(2)}, u32[]{:S(2)}) async-start(f32[3,8,12,512]{3,2,0,1:T(8,128)} %copy.80), calls=%async_computation | async-start | bytes 1572864 | tf_op jit(solution)/shard_map/all_to_all | solution.py:80
  472.2 176.2 %all-reduce.5.cloned.1.call-start = ((), (), s32[]{:S(2)}) async-start(), calls=%async_computation.12 | async-start | bytes 12582912 | tf_op jit(solution)/shard_map/psum | solution.py:56
  497.8 25.3 %all-to-all-start.1 = ((f32[16,3,1,12,512]{4,2,3,1,0:T(1,128)}), f32[16,3,1,12,512]{4,2,3,1,0:T(1,128)}, u32[]{:S(2)}, u32[]{:S(2)}) async-start(f32[16,3,1,12,512]{4,2,3,1,0:T(1,128)} %fusion.49), calls=%async_computation.1 | async-start | bytes 2359296 | tf_op jit(solution)/shard_map/all_to_all | solution.py:89
  525.6 11.3 %copy-start.17 = (f32[96,512]{1,0:T(8,128)S(1)}, f32[96,512]{1,0:T(8,128)}, u32[]{:S(2)}) copy-start(f32[96,512]{1,0:T(8,128)} %fusion.4) | copy-start | bytes 589828
  525.6 19.7 %all-to-all-start.2 = ((f32[3,8,12,512]{3,2,0,1:T(8,128)}), f32[3,8,12,512]{3,2,0,1:T(8,128)}, u32[]{:S(2)}, u32[]{:S(2)}) async-start(f32[3,8,12,512]{3,2,0,1:T(8,128)} %bitcast.230), calls=%async_computation.2 | async-start | bytes 1572864 | tf_op jit(solution)/shard_map/all_to_all | solution.py:92
  652.2 5.8 copy-start.1
  652.2 3.8 copy-start.8
  652.2 3.8 copy-start.9
  654.1 3.9 copy-start.10
  654.1 3.9 copy-start.11
  656.0 12.5 %copy-start.3 = (f32[512,512]{0,1:T(8,128)}, f32[512,512]{0,1:T(8,128)S(1)}, u32[]{:S(2)}) copy-start(f32[512,512]{0,1:T(8,128)S(1)} %fusion.18) | copy-start | bytes 3145732
  658.0 5.1 copy-start.6
  660.0 1.0 copy-start.7
  663.1 5.4 copy-start.4
  680.8 4.3 copy-start.2
  680.8 4.3 copy-start.12
  680.8 4.3 copy-start.15
  685.1 1.2 copy-start.13
  685.1 1.5 copy-start.14
  686.7 1.9 copy-start.5
Sparse Core Ops, SparseCore 0:
  10.7 46.3 all-gather.5
  59.2 43.3 all-gather.3
  104.7 43.3 all-gather.7
  151.0 65.1 all-reduce.6
  225.4 75.7 reduce-scatter.9
  304.4 75.1 reduce-scatter.11
  383.4 75.0 reduce-scatter.13
  479.0 169.3 all-reduce.4
